TPU v7x, 256 devices: a whole 4x4x8 slice. The times are simulated.
256 devices in a mesh: ctx: 16 (over z, x_hi), head: 16 (over x_lo, y, core).
Axes of the slice: x: 4 (x_hi: 2, x_lo: 2; x = x_hi * 2 + x_lo), y: 4, z: 8, core: 2. Of those that a mesh axis runs over, the one named last changes fastest.
Arguments:
- hidden: bfloat16 [16384, 8192], P('ctx', 'head'), may hold values from -6 to 6
- query_frozen_projection: bfloat16 [16384, 8192], P('ctx', 'head'), may hold values from -20 to 20
- key_projected: bfloat16 [16384, 1024], P('ctx'), may hold values from -20 to 20
- value_frozen_projection: bfloat16 [16384, 1024], P('ctx'), may hold values from -6 to 6
- query_down_factor: bfloat16 [8192, 16], P('head'), may hold values from -0.0625 to 0.0625
- query_up_factor: bfloat16 [16, 8192], P(None, 'head'), may hold values from -1.5 to 1.5
- value_down_factor: bfloat16 [8192, 16], P('head'), may hold values from -0.0625 to 0.0625
- value_up_factor: bfloat16 [16, 1024], replicated, may hold values from -1.5 to 1.5
- output_gradient: bfloat16 [16384, 8192], P('ctx', 'head'), may hold values from -0.046875 to 0.046875
- head_shift_mask: int32 [64], P('head'), may hold values from 0 to 1, as said below
Outputs:
- grad_a_q: float32 [8192, 16], P('head')
- query_up_gradient: float32 [16, 8192], P(None, 'head')
- grad_a_v: float32 [8192, 16], P('head')
- value_up_gradient: float32 [16, 1024], replicated
Inputs may be any that keep to these rules, and one draw needn't show every extreme that they name: `head_shift_mask`: exactly 32 of the heads carry 1.
All inputs are finite; a program needn't handle non-finite values.
Results may differ from a plain program's by a relative error of at most 0.0173.
The roundings to bfloat16 on the way count: a program that leaves them out, or rounds other values in their place, can miss the bound.
Values may be sent and summed in bfloat16 or wider, within the bound.
A program may use at most 128 MiB of HBM per device.

v0:
```python
import jax
import jax.numpy as jnp
from jax import lax
from jax.sharding import PartitionSpec as P

QUERY_HEADS = 64
KEY_VALUE_HEADS = 8
HEAD_SIZE = 128


adapter_scale = 2.0
pos_interp = 32.0
rope_base = 10000.0


def passed_along(block, axis, distance):
    devices = range(lax.axis_size(axis))
    route = [((i - distance) % len(devices), i) for i in devices]
    return lax.ppermute(block, axis, route)


def rope_tables(positions, head_width):
    half_width = head_width // 2
    inv_freq = rope_base ** (-(jnp.arange(half_width, dtype=jnp.float32) * 2.0 / head_width))
    angles = (positions.astype(jnp.float32) / pos_interp)[:, None] * inv_freq[None, :]
    return (jnp.cos(angles), jnp.sin(angles))


def rotate(tensor, cosine, sine_table):
    half_width = tensor.shape[-1] // 2
    first_half = tensor[..., :half_width]
    second_half = tensor[..., half_width:]
    return jnp.concatenate(
        [
            first_half * cosine - second_half * sine_table,
            second_half * cosine + first_half * sine_table,
        ],
        axis=-1,
    )


def unrotate(tensor, cosine, sine_table):
    half_width = tensor.shape[-1] // 2
    first_half = tensor[..., :half_width]
    second_half = tensor[..., half_width:]
    return jnp.concatenate(
        [
            first_half * cosine + second_half * sine_table,
            second_half * cosine - first_half * sine_table,
        ],
        axis=-1,
    )


def group_grads(query_rows, key_rows, value_rows, upstream):
    scale_factor = query_rows.shape[-1] ** (-0.5)
    scores = jnp.dot(query_rows, key_rows.T, preferred_element_type=jnp.float32) * scale_factor
    row_ids = lax.broadcasted_iota(jnp.int32, scores.shape, 0)
    col_ids = lax.broadcasted_iota(jnp.int32, scores.shape, 1)
    scores = jnp.where(col_ids <= row_ids, scores, -1e30)
    row_peak = jnp.max(scores, axis=1, keepdims=True)
    weights = jnp.exp(scores - row_peak)
    probs = weights / jnp.sum(weights, axis=1, keepdims=True)
    probs_low = probs.astype(jnp.bfloat16)
    output = jnp.dot(probs_low, value_rows, preferred_element_type=jnp.float32)
    delta = jnp.sum(upstream.astype(jnp.float32) * output, axis=1, keepdims=True)
    prob_grad = jnp.dot(upstream, value_rows.T, preferred_element_type=jnp.float32)
    score_grad = (probs * (prob_grad - delta)).astype(jnp.bfloat16)
    query_grad = jnp.dot(score_grad, key_rows, preferred_element_type=jnp.float32) * scale_factor
    value_gradient_total = jnp.dot(probs_low.T, upstream, preferred_element_type=jnp.float32)
    return (query_grad, value_gradient_total)


def regroup(own_rows, next_rows, head_mask):
    half_rows = next_rows.shape[0]
    shifted = jnp.concatenate([own_rows[half_rows:], next_rows], axis=0)
    return jnp.where(head_mask, shifted, own_rows)


def split_rows(gradient, head_mask, half_rows):
    lower_rows = gradient[:, :half_rows]
    upper_rows = gradient[:, half_rows:]
    own_part = jnp.where(
        head_mask, jnp.concatenate([jnp.zeros_like(lower_rows), lower_rows], axis=1), gradient
    )
    send_part = jnp.where(head_mask, upper_rows, jnp.zeros_like(upper_rows))
    return (own_part, send_part)


def on_device(
    hidden,
    query_frozen_projection,
    key_projected,
    value_frozen_projection,
    query_down_factor,
    query_up_factor,
    value_down_factor,
    value_up_factor,
    output_gradient,
    head_shift_mask,
):
    highest_precision = lax.Precision.HIGHEST
    group_rows = hidden.shape[0]
    half_rows = group_rows // 2
    heads_here = head_shift_mask.shape[0]
    adapter_rank_width = query_down_factor.shape[1]
    per_kv = QUERY_HEADS // KEY_VALUE_HEADS
    local_key_value_heads = max(1, heads_here // per_kv)
    fan_out = heads_here // local_key_value_heads
    ctx_number = lax.axis_index("ctx")
    head_number = lax.axis_index("head")
    first_key_value_head = head_number * heads_here // per_kv
    query_partial_sum = jnp.dot(hidden, query_down_factor, preferred_element_type=jnp.float32)
    value_partial_sum = jnp.dot(hidden, value_down_factor, preferred_element_type=jnp.float32)
    summed_q, summed_v = lax.psum((query_partial_sum, value_partial_sum), "head")
    query_upstream = summed_q.astype(jnp.bfloat16)
    value_upstream = summed_v.astype(jnp.bfloat16)
    own_pos = ctx_number * group_rows + jnp.arange(group_rows, dtype=jnp.int32)
    cosine, sine_table = rope_tables(own_pos, HEAD_SIZE)
    cos_rows = cosine[:, None, :]
    sin_rows = sine_table[:, None, :]
    query_before_rotary = query_frozen_projection.astype(jnp.float32) + adapter_scale * jnp.dot(
        query_upstream.astype(jnp.float32),
        query_up_factor.astype(jnp.float32),
        precision=highest_precision,
    )
    query_rows = rotate(
        query_before_rotary.reshape(group_rows, heads_here, HEAD_SIZE), cos_rows, sin_rows
    ).astype(jnp.bfloat16)
    key_cols = lax.dynamic_slice_in_dim(
        key_projected, first_key_value_head * HEAD_SIZE, local_key_value_heads * HEAD_SIZE, 1
    )
    key_rows = rotate(
        key_cols.astype(jnp.float32).reshape(group_rows, local_key_value_heads, HEAD_SIZE),
        cos_rows,
        sin_rows,
    ).astype(jnp.bfloat16)
    value_up_local = lax.dynamic_slice_in_dim(
        value_up_factor, first_key_value_head * HEAD_SIZE, local_key_value_heads * HEAD_SIZE, 1
    )
    value_columns = lax.dynamic_slice_in_dim(
        value_frozen_projection,
        first_key_value_head * HEAD_SIZE,
        local_key_value_heads * HEAD_SIZE,
        1,
    )
    value_before_adapter = value_columns.astype(jnp.float32) + adapter_scale * jnp.dot(
        value_upstream.astype(jnp.float32),
        value_up_local.astype(jnp.float32),
        precision=highest_precision,
    )
    value_rows = value_before_adapter.astype(jnp.bfloat16).reshape(
        group_rows, local_key_value_heads, HEAD_SIZE
    )
    upstream = output_gradient.reshape(group_rows, heads_here, HEAD_SIZE)
    head_flags = head_shift_mask > 0
    token_mask = head_flags[None, :, None]
    stack_mask = head_flags[:, None, None]
    next_query, next_keys, next_values, next_upstream = passed_along(
        (
            query_rows[:half_rows],
            key_rows[:half_rows],
            value_rows[:half_rows],
            upstream[:half_rows],
        ),
        "ctx",
        -1,
    )
    group_query = regroup(query_rows, next_query, token_mask)
    group_keys = regroup(
        jnp.repeat(key_rows, fan_out, axis=1), jnp.repeat(next_keys, fan_out, axis=1), token_mask
    )
    group_values = regroup(
        jnp.repeat(value_rows, fan_out, axis=1),
        jnp.repeat(next_values, fan_out, axis=1),
        token_mask,
    )
    group_upstream = regroup(upstream, next_upstream, token_mask)
    stacked = (
        jnp.moveaxis(group_query, 1, 0),
        jnp.moveaxis(group_keys, 1, 0),
        jnp.moveaxis(group_values, 1, 0),
        jnp.moveaxis(group_upstream, 1, 0),
    )
    query_grads, value_grads = lax.map(
        lambda members: group_grads(members[0], members[1], members[2], members[3]), stacked
    )
    own_query, send_query = split_rows(query_grads, stack_mask, half_rows)
    own_value, send_value = split_rows(value_grads, stack_mask, half_rows)
    own_value_kv = own_value.reshape(local_key_value_heads, fan_out, group_rows, HEAD_SIZE).sum(
        axis=1
    )
    send_value_kv = send_value.reshape(local_key_value_heads, fan_out, half_rows, HEAD_SIZE).sum(
        axis=1
    )
    back_query, back_value = passed_along((send_query, send_value_kv), "ctx", 1)
    own_query = own_query.at[:, :half_rows].add(back_query)
    own_value_kv = own_value_kv.at[:, :half_rows].add(back_value)
    prior_gradient = unrotate(jnp.moveaxis(own_query, 0, 1), cos_rows, sin_rows).reshape(
        group_rows, heads_here * HEAD_SIZE
    )
    value_token_rows = jnp.moveaxis(own_value_kv, 0, 1).reshape(
        group_rows, local_key_value_heads * HEAD_SIZE
    )
    query_up_gradient_piece = adapter_scale * jnp.dot(
        query_upstream.astype(jnp.float32).T, prior_gradient, precision=highest_precision
    )
    value_gradient_piece = adapter_scale * jnp.dot(
        value_upstream.astype(jnp.float32).T, value_token_rows, precision=highest_precision
    )
    token_query_piece = adapter_scale * jnp.dot(
        prior_gradient, query_up_factor.astype(jnp.float32).T, precision=highest_precision
    )
    token_value_piece = adapter_scale * jnp.dot(
        value_token_rows, value_up_local.astype(jnp.float32).T, precision=highest_precision
    )
    value_full = lax.dynamic_update_slice_in_dim(
        jnp.zeros((adapter_rank_width, KEY_VALUE_HEADS * HEAD_SIZE), jnp.float32),
        value_gradient_piece,
        first_key_value_head * HEAD_SIZE,
        1,
    )
    token_query_gradient, token_value_gradient = lax.psum(
        (token_query_piece, token_value_piece), "head"
    )
    a_q_part = jnp.dot(
        hidden.T, token_query_gradient.astype(jnp.bfloat16), preferred_element_type=jnp.float32
    )
    a_v_part = jnp.dot(
        hidden.T, token_value_gradient.astype(jnp.bfloat16), preferred_element_type=jnp.float32
    )
    grad_a_q, grad_a_v, query_up_gradient = lax.psum(
        (a_q_part, a_v_part, query_up_gradient_piece), "ctx"
    )
    value_up_gradient = lax.psum(value_full, ("ctx", "head"))
    return (grad_a_q, query_up_gradient, grad_a_v, value_up_gradient)


def solution(mesh):
    return jax.shard_map(
        on_device,
        mesh=mesh,
        in_specs=(
            P("ctx", "head"),
            P("ctx", "head"),
            P("ctx", None),
            P("ctx", None),
            P("head", None),
            P(None, "head"),
            P("head", None),
            P(),
            P("ctx", "head"),
            P("head"),
        ),
        out_specs=(P("head", None), P(None, "head"), P("head", None), P()),
        check_vma=False,
    )
```

profile of v0, /device:TPU:8, one launch (start us, length us, event | category | flops | bytes accessed | tf_op | source)
XLA Modules:
  0.0 588.5 jit_solution(2511384332108965878)
XLA Ops:
  8.4 2.4 fusion.51
  11.6 8.3 %collective-permute-start.1 = (bf16[512,1,128]{2,0,1:T(8,128)(2,1)}, bf16[512,1,128]{2,0,1:T(8,128)(2,1)}, u32[]{:S(2)}, u32[]{:S(2)}) collective-permute-start(bf16[512,1,128]{2,0,1:T(8,128)(2,1)} %pad_maximum_fusion.3), channel_id=1, source_target_pairs={{16,0},{32,16},{48,32},{64,48},{80,64},{96,80},{112,96},{128,112},... | collective-permute-start | bytes 393224 | tf_op jit(solution)/shard_map/ppermute | solution.py:19
  19.9 1.8 multiply_cosine_fusion.1
  23.0 52.5 %all-reduce.13 = (bf16[1024,16]{0,1:T(8,128)(2,1)S(1)}, bf16[1024,16]{0,1:T(8,128)(2,1)}) all-reduce(f32[1024,16]{0,1:T(8,128)S(1)} %fusion.72, f32[1024,16]{0,1:T(8,128)S(1)} %fusion.73), channel_id=1, replica_groups=mesh['ctx'=16,'head'=16] {'head'}, use_global_device_ids=true, to_apply=%region_0.1 | all-reduce | flops 32768 | bytes 196608 | tf_op jit(solution)/shard_map/psum | solution.py:115
  78.1 2.0 collective-permute-start
  82.6 2.0 collective-permute-start.2
  87.3 2.0 collective-permute-start.3
  89.3 1.8 copy.47
  95.5 1.8 copy.41
  101.9 2.0 collective-permute-done.3
  108.5 4.5 fusion.45
  113.1 45.1 %while.14 = (s32[]{:T(128)}, f32[4,1024,128]{1,2,0:T(8,128)}, f32[4,1024,128]{1,2,0:T(8,128)}, bf16[4,1024,128]{1,2,0:T(8,128)(2,1)}, bf16[4,1024,128]{1,2,0:T(8...) while((s32[]{:T(128)}, f32[4,1024,128]{1,2,0:T(8,128)}, ...), condition=%wide.region_6.7_spmd, body=%wide.region_2.6_spmd.sunk | while | flops 1373107200 | bytes 51430568 | solution.py:185
  113.1 1.8 fusion.111
  119.3 4.0 fusion.114
  130.6 4.0 fusion.114
  141.9 4.0 fusion.114
  153.2 4.0 fusion.114
  158.2 3.8 select_reduce_fusion.1
  162.0 2.0 collective-permute-start.4
  164.8 10.0 %collective-permute-done.5 = f32[1,512,128]{1,2,0:T(8,128)S(1)} collective-permute-done((f32[1,512,128]{1,2,0:T(8,128)S(1)}, f32[1,512,128]{1,2,0:T(8,128)S(1)}, u32[]{:S(2)}, u32[]{:S(2)}) %collective-permute-start.5) | collective-permute-done | bytes 262176 | tf_op jit(solution)/shard_map/ppermute | solution.py:19
  178.4 13.2 %collective-permute-done.4 = f32[4,512,128]{1,2,0:T(8,128)} collective-permute-done((f32[4,512,128]{1,2,0:T(8,128)}, f32[4,512,128]{1,2,0:T(8,128)}, u32[]{:S(2)}, u32[]{:S(2)}) %collective-permute-start.4) | collective-permute-done | bytes 1048608 | tf_op jit(solution)/shard_map/ppermute | solution.py:19
  196.2 61.3 %all-reduce.14 = (bf16[1024,16]{0,1:T(8,128)(2,1)S(1)}, bf16[1024,16]{0,1:T(8,128)(2,1)S(1)}) all-reduce(f32[1024,16]{0,1:T(8,128)S(1)} %convolution_multiply_fusion.2, f32[1024,16]{0,1:T(8,128)S(1)} %convolution_multiply_fusion.3), channel_id=1, replica_groups=mesh['ctx'=16,'head'=16] {'head'}, use_global_device_ids=true, to_apply=%region_7.8 | all-reduce | flops 32768 | bytes 196608 | tf_op jit(solution)/shard_map/psum | solution.py:223
  259.3 158.1 %all-reduce.10.cloned.1.call-done = f32[16,1024]{1,0:T(8,128)} async-done(((f32[16,1024]{1,0:T(8,128)}), f32[16,1024]{1,0:T(8,128)}) %all-reduce.10.cloned.1.call-update) | async-done | bytes 65552 | tf_op jit(solution)/shard_map/psum | solution.py:235
  417.4 158.7 %all-reduce.12.cloned.1.call-done = (f32[512,16]{0,1:T(8,128)}, f32[16,512]{1,0:T(8,128)}, f32[512,16]{0,1:T(8,128)}) async-done(((f32[512,16]{0,1:T(8,128)}, f32[16,512]{1,0:T(8,128)}, f32[512,16]{0,1:T(8,128)}), (f32[512,16]{0,1:T(8,128)}, f32[16,512]{1,0:T(8,128)}, f32[512,16]{0,1:T(8,128)})) %all-reduce.12.cloned.1.call-update) | async-done | bytes 98320 | tf_op jit(solution)/shard_map/psum | solution.py:232
  (148 shorter events, 68.0 us)
Async XLA Ops:
  7.2 14.5 %copy-start = (bf16[1024,512]{1,0:T(8,128)(2,1)S(1)}, bf16[1024,512]{1,0:T(8,128)(2,1)}, u32[]{:S(2)}) copy-start(bf16[1024,512]{1,0:T(8,128)(2,1)} %param.16) | copy-start | bytes 3145732
  7.2 14.5 %copy-start.24 = (bf16[512,16]{0,1:T(8,128)(2,1)S(1)}, bf16[512,16]{0,1:T(8,128)(2,1)}, u32[]{:S(2)}) copy-start(bf16[512,16]{0,1:T(8,128)(2,1)} %param.20) | copy-start | bytes 49156
  7.2 410.2 %all-reduce.10.cloned.1.call-start = ((), (), s32[]{:S(2)}) async-start(), calls=%async_computation | async-start | bytes 131072 | tf_op jit(solution)/shard_map/psum | solution.py:235
  8.4 13.7 %copy-start.25 = (bf16[512,16]{0,1:T(8,128)(2,1)S(1)}, bf16[512,16]{0,1:T(8,128)(2,1)}, u32[]{:S(2)}) copy-start(bf16[512,16]{0,1:T(8,128)(2,1)} %param.22) | copy-start | bytes 49156
  10.8 11.3 %copy-start.5 = (bf16[1024,1,64]{2,0,1:T(8,128)(2,1)}, bf16[1024,1,64]{2,0,1:T(8,128)(2,1)S(1)}, u32[]{:S(2)}) copy-start(bf16[1024,1,64]{2,0,1:T(8,128)(2,1)S(1)} %get-tuple-element.118) | copy-start | bytes 393220
  10.8 11.7 %copy-start.15 = (bf16[1024,512]{1,0:T(8,128)(2,1)S(1)}, bf16[1024,512]{1,0:T(8,128)(2,1)}, u32[]{:S(2)}) copy-start(bf16[1024,512]{1,0:T(8,128)(2,1)} %param.17) | copy-start | bytes 3145732
  11.6 88.6 %collective-permute-start.1 = (bf16[512,1,128]{2,0,1:T(8,128)(2,1)}, bf16[512,1,128]{2,0,1:T(8,128)(2,1)}, u32[]{:S(2)}, u32[]{:S(2)}) collective-permute-start(bf16[512,1,128]{2,0,1:T(8,128)(2,1)} %pad_maximum_fusion.3), channel_id=1, source_target_pairs={{16,0},{32,16},{48,32},{64,48},{80,64},{96,80},{112,96},{128,112},... | collective-permute-start | bytes 393224 | tf_op jit(solution)/shard_map/ppermute | solution.py:19
  21.7 53.8 %copy-start.23 = (bf16[16,512]{1,0:T(8,128)(2,1)S(1)}, bf16[16,512]{1,0:T(8,128)(2,1)}, u32[]{:S(2)}) copy-start(bf16[16,512]{1,0:T(8,128)(2,1)} %param.21) | copy-start | bytes 49156
  78.1 6.5 %copy-start.21 = (bf16[1024,16]{0,1:T(8,128)(2,1)S(1)}, bf16[1024,16]{0,1:T(8,128)(2,1)}, u32[]{:S(2)}) copy-start(bf16[1024,16]{0,1:T(8,128)(2,1)} %get-tuple-element.99) | copy-start | bytes 98308
  78.1 27.4 %collective-permute-start = (bf16[512,4,128]{0,2,1:T(8,128)(2,1)}, bf16[512,4,128]{0,2,1:T(8,128)(2,1)}, u32[]{:S(2)}, u32[]{:S(2)}) collective-permute-start(bf16[512,4,128]{0,2,1:T(8,128)(2,1)} %get-tuple-element.116), channel_id=1, source_target_pairs={{16,0},{32,16},{48,32},{64,48},{80,64},{96,80},{112,96},{128,112},... | collective-permute-start | bytes 1572872 | tf_op jit(solution)/shard_map/ppermute | solution.py:19
  82.6 22.9 %collective-permute-start.2 = (bf16[512,4,128]{0,2,1:T(8,128)(2,1)}, bf16[512,4,128]{0,2,1:T(8,128)(2,1)}, u32[]{:S(2)}, u32[]{:S(2)}) collective-permute-start(bf16[512,4,128]{0,2,1:T(8,128)(2,1)} %bitcast.15), channel_id=1, source_target_pairs={{16,0},{32,16},{48,32},{64,48},{80,64},{96,80},{112,96},{128,112},... | collective-permute-start | bytes 1572872 | tf_op jit(solution)/shard_map/ppermute | solution.py:19
  87.3 16.6 %collective-permute-start.3 = (bf16[512,1,128]{2,0,1:T(8,128)(2,1)}, bf16[512,1,128]{2,0,1:T(8,128)(2,1)}, u32[]{:S(2)}, u32[]{:S(2)}) collective-permute-start(bf16[512,1,128]{2,0,1:T(8,128)(2,1)} %get-tuple-element.120), channel_id=1, source_target_pairs={{16,0},{32,16},{48,32},{64,48},{80,64},{96,80},{112,96},{128,112},... | collective-permute-start | bytes 393224 | tf_op jit(solution)/shard_map/ppermute | solution.py:19
  95.5 13.0 %copy-start.13 = (bf16[1024,128]{0,1:T(8,128)(2,1)S(1)}, bf16[1024,128]{0,1:T(8,128)(2,1)}, u32[]{:S(2)}) copy-start(bf16[1024,128]{0,1:T(8,128)(2,1)} %copy.47) | copy-start | bytes 786436
  113.1 45.1 %copy-start.27 = (pred[4]{0:T(512)(128)(4,1)S(1)}, pred[4]{0:T(512)(128)(4,1)}, u32[]{:S(2)}) copy-start(pred[4]{0:T(512)(128)(4,1)} %broadcast_compare_fusion) | copy-start | bytes 16
  114.9 3.7 copy-start.1
  148.7 3.7 copy-start.1
  158.2 5.8 copy-start.2
  158.2 5.8 copy-start.3
  162.0 12.8 %collective-permute-start.5 = (f32[1,512,128]{1,2,0:T(8,128)S(1)}, f32[1,512,128]{1,2,0:T(8,128)S(1)}, u32[]{:S(2)}, u32[]{:S(2)}) collective-permute-start(f32[1,512,128]{1,2,0:T(8,128)S(1)} %bitcast.125), channel_id=1, source_target_pairs={{240,0},{0,16},{16,32},{32,48},{48,64},{64,80},{80,96},{96,112},{1... | collective-permute-start | bytes 786440 | tf_op jit(solution)/shard_map/ppermute | solution.py:19
  162.0 29.6 %collective-permute-start.4 = (f32[4,512,128]{1,2,0:T(8,128)}, f32[4,512,128]{1,2,0:T(8,128)}, u32[]{:S(2)}, u32[]{:S(2)}) collective-permute-start(f32[4,512,128]{1,2,0:T(8,128)} %get-tuple-element.124), channel_id=1, source_target_pairs={{240,0},{0,16},{16,32},{32,48},{48,64},{64,80},{80,96},{96,112},{1... | collective-permute-start | bytes 3145736 | tf_op jit(solution)/shard_map/ppermute | solution.py:19
  164.0 11.6 %copy-start.22 = (bf16[1024,16]{0,1:T(8,128)(2,1)S(1)}, bf16[1024,16]{0,1:T(8,128)(2,1)}, u32[]{:S(2)}) copy-start(bf16[1024,16]{0,1:T(8,128)(2,1)} %get-tuple-element.99) | copy-start | bytes 98308
  175.7 17.5 %copy-start.7 = (f32[1024,64]{0,1:T(8,128)S(1)}, f32[1024,64]{0,1:T(8,128)}, u32[]{:S(2)}) copy-start(f32[1024,64]{0,1:T(8,128)} %get-tuple-element.121) | copy-start | bytes 786436
  176.7 399.4 %all-reduce.12.cloned.1.call-start = ((), (), s32[]{:S(2)}) async-start(), calls=%async_computation.1 | async-start | bytes 196608 | tf_op jit(solution)/shard_map/psum | solution.py:232
  177.0 16.2 %copy-start.9 = (f32[1024,64]{0,1:T(8,128)S(1)}, f32[1024,64]{0,1:T(8,128)}, u32[]{:S(2)}) copy-start(f32[1024,64]{0,1:T(8,128)} %get-tuple-element.122) | copy-start | bytes 786436
  (21 other events, 39.9 us)
Sparse Core Ops, SparseCore 0:
  176.8 240.5 all-reduce.9
  420.8 155.2 all-reduce.11
where the time goes:
time: 590 us; the launch traced here: 589 us
  waiting for transfers between devices  342 us (58%)
  blocking collectives  114 us (19%)
  matrix products  41.3 us (7%)
  local copies, waits for them, and re-layouts  34.7 us (6%)
  other arithmetic  25.5 us (4%)
  starting transfers between devices  16.6 us (3%)
  between operations  14.4 us (2%)
    psum x1, waiting for transfers between devices, on_device(): lax.psum((a_q_part, a_v_part, query_up_gradient_piece), 'ctx')  159 us
    psum x1, waiting for transfers between devices, on_device(): value_up_gradient = lax.psum(value_full, ('ctx', 'head'))  158 us
    psum x1, blocking collectives, on_device(): lax.psum((token_query_piece, token_value_piece), 'head')  61.3 us
    psum x1, blocking collectives, on_device(): lax.psum((query_partial_sum, value_partial_sum), 'head')  52.5 us
    ppermute x6, waiting for transfers between devices, passed_along(): return lax.ppermute(block, axis, route)  25.2 us
    ppermute x6, starting transfers between devices, passed_along(): return lax.ppermute(block, axis, route)  16.3 us
    dot_general x4, matrix products, group_grads(): jnp.dot(score_grad, key_rows, preferred_element_type=jnp.float32)  15.8 us
  transfers between devices with their start and end apart: 8, of which 5 were waited for; matrix products, arithmetic and copies ran while one was open for 6% of the time, Pallas kernels for 0%

commit v1 on v0

v1 whole, which is shorter than its diff:
```python
import functools

import jax
import jax.numpy as jnp
import numpy as np
from jax import lax
from jax.experimental import pallas as pl
from jax.experimental.pallas import tpu as pltpu
from jax.sharding import PartitionSpec as P

QUERY_HEADS = 64
KEY_VALUE_HEADS = 8
HEAD_SIZE = 128

adapter_scale = 2.0
pos_interp = 32.0
rope_base = 10000.0
LOG2E = 1.4426950408889634
MESH = pl.DeviceIdType.MESH
BLK = 256
HALF_HEAD = HEAD_SIZE // 2
BF = jnp.bfloat16
F32 = jnp.float32


def angle_tables(rows, groups):
    inv_freq = rope_base ** (-(np.arange(HALF_HEAD, dtype=np.float64) * 2.0 / HEAD_SIZE))
    fine = inv_freq[:, None] * (np.arange(rows, dtype=np.float64) / pos_interp)[None, :]
    coarse = inv_freq[:, None] * (np.arange(128, dtype=np.float64) * rows / pos_interp)[None, :]
    make = lambda f, x: np.asarray(f(x), dtype=np.float32)
    return make(np.cos, fine), make(np.sin, fine), make(np.cos, coarse), make(np.sin, coarse)


def nn(a, b):
    return lax.dot_general(a, b, (((1,), (0,)), ((), ())), preferred_element_type=F32)


def nt(a, b):
    return lax.dot_general(a, b, (((1,), (1,)), ((), ())), preferred_element_type=F32)


def tn(a, b):
    return lax.dot_general(a, b, (((0,), (0,)), ((), ())), preferred_element_type=F32)


def turned(x, c, s):
    top, low = x[:HALF_HEAD], x[HALF_HEAD:]
    return jnp.concatenate([top * c - low * s, low * c + top * s], axis=0)


def turned_back(x, c, s):
    top, low = x[:HALF_HEAD], x[HALF_HEAD:]
    return jnp.concatenate([top * c + low * s, low * c - top * s], axis=0)


def kernel(
    nc, nh, heads,
    hid, qf, kp, vf, qd, qu, vd, vu, dog, msk, fine_c, fine_s, coarse_c, coarse_s,
    o_aq, o_qu, o_av, o_vu,
    hidv, qfv, dov, kvown, kvprev, dnv, quv, vul, fc, fs, cc, cs,
    ub, ur, us, ug, uvp,
    qt, dt, dn, kk, kt, vv, tc, ts, tcp, tsp, uq, uv,
    tq, qacc, dv,
    tsend, trecv, tprev, tsum, tg,
    es, er, esum, eg, vg,
    gs, gr, gsum, gg,
    lsem, kvs, kvr, fws, fwr, ups, upr,
    urs_s, urs_r, uag_s, uag_r, trs_s, trs_r, tps_s, tps_r, tag_s, tag_r,
    ers_s, ers_r, eag_s, eag_r, vag_s, vag_r, grs_s, grs_r, gag_s, gag_r,
):
    c, h = lax.axis_index("ctx"), lax.axis_index("head")
    nxt, prv = lax.rem(c + 1, nc), lax.rem(c + nc - 1, nc)
    core = lax.rem(h, 2)
    sib = h + 1 - 2 * core
    kvh = h * heads // (QUERY_HEADS // KEY_VALUE_HEADS)
    kvcol = pl.ds(pl.multiple_of(kvh * HEAD_SIZE, HEAD_SIZE), HEAD_SIZE)
    m = 16 // nc

    local = [
        (hid, hidv), (kp.at[:, kvcol], kvown.at[0]), (vf.at[:, kvcol], kvown.at[1]),
        (qd, dnv.at[0]), (vd, dnv.at[1]), (fine_c, fc), (fine_s, fs), (coarse_c, cc), (coarse_s, cs),
        (qf, qfv), (dog, dov), (qu, quv), (vu.at[:, kvcol], vul),
    ]
    copies = [pltpu.make_async_copy(a, b, lsem.at[i]) for i, (a, b) in enumerate(local)]
    for i in (0, 3, 4, 1, 2, 5, 6, 7, 8, 10, 9, 11, 12):
        copies[i].start()

    bar = pltpu.get_barrier_semaphore()

    def greet(dev):
        pl.semaphore_signal(bar, inc=1, device_id=dev, device_id_type=MESH)

    @pl.loop(1, nh)
    def _(i):
        p = lax.rem(h + i, nh)
        greet((c, p))
        greet((nxt, p))
        greet((prv, p))

    @pl.loop(1, nc)
    def _(i):
        greet((lax.rem(c + i, nc), h))

    def rdma(src, dst, ssem, rsem, dev):
        return pltpu.make_async_remote_copy(
            src_ref=src, dst_ref=dst, send_sem=ssem, recv_sem=rsem, device_id=dev, device_id_type=MESH
        )

    def each(n, me, f):
        @pl.loop(1, n)
        def _(i):
            f(lax.rem(me + i, n))

    def head_rs(src, dst, ssem, rsem, p):
        return rdma(src.at[p], dst.at[h], ssem.at[p], rsem.at[h], (c, p))

    def head_from(dst, ssem, rsem, p):
        return rdma(dst.at[p], dst.at[p], ssem.at[p], rsem.at[p], (c, p))

    def head_ag(src, dst, ssem, rsem, p):
        return rdma(src, dst.at[h], ssem.at[p], rsem.at[h], (c, p))

    def ctx_from(dst, ssem, rsem, p):
        return rdma(dst.at[p], dst.at[p], ssem.at[p], rsem.at[p], (p, h))

    for i in (0, 3, 4):
        copies[i].wait()
    ut = nt(dnv[...].reshape(32, dnv.shape[2]), hidv[...])
    for p in range(16):
        r, l = p // 8, p % 8
        ub[p] = ut[16 * r:16 * r + 16, 128 * l:128 * l + 128]
    pl.semaphore_wait(bar, 3 * (nh - 1) + nc - 1)
    each(nh, h, lambda p: head_rs(ub, ur, urs_s, urs_r, p).start())

    copies[1].wait()
    copies[2].wait()
    half = kvown.shape[1] // 2
    kv_send = rdma(kvown.at[core, pl.ds(half, half)], kvprev.at[core], kvs, kvr, (nxt, h))
    kv_send.start()

    for i in (5, 6, 7, 8):
        copies[i].wait()
    lane = lax.broadcasted_iota(jnp.int32, cc.shape, 1)

    def column(tab, at):
        return jnp.sum(jnp.where(lane == at, tab, 0.0), axis=1, keepdims=True)

    def tables(at, blocks, c_ref, s_ref):
        base_c, base_s = column(cc[...], at), column(cs[...], at)
        for j, b in enumerate(blocks):
            f_c, f_s = fc[:, BLK * b:BLK * b + BLK], fs[:, BLK * b:BLK * b + BLK]
            c_ref[j] = base_c * f_c - base_s * f_s
            s_ref[j] = base_s * f_c + base_c * f_s

    tables(c, (0, 1, 2, 3), tc, ts)
    tables(prv, (2, 3), tcp, tsp)

    def key_block(raw, b, cos, sin):
        k_t = turned(raw.astype(F32).T, cos, sin).astype(BF)
        kt[b] = k_t
        kk[b] = k_t.astype(F32).T.astype(BF)

    for b in range(4):
        key_block(kvown[0, BLK * b:BLK * b + BLK], b, tc[b], ts[b])

    ur[h] = ub[h]
    each(nh, h, lambda p: head_from(ur, urs_s, urs_r, p).wait_recv())
    u_sum = ur[0]
    for p in range(1, 16):
        u_sum = u_sum + ur[p]
    us[...] = u_sum.astype(BF)
    ug[h] = us[...]
    each(nh, h, lambda p: head_ag(us, ug, uag_s, uag_r, p).start())

    copies[10].wait()
    for hd in range(heads):
        for b in range(4):
            x = dov[BLK * b:BLK * b + BLK, HEAD_SIZE * hd:HEAD_SIZE * (hd + 1)]
            dn[hd, b] = x
            dt[hd, b] = x.astype(F32).T.astype(BF)
    copies[9].wait()
    for hd in range(heads):
        for b in range(4):
            x = qfv[BLK * b:BLK * b + BLK, HEAD_SIZE * hd:HEAD_SIZE * (hd + 1)]
            qt[hd, b] = x.astype(F32).T.astype(BF)
    tq[...] = jnp.zeros_like(tq)
    dv[...] = jnp.zeros_like(dv)
    copies[11].wait()
    copies[12].wait()

    each(nh, h, lambda p: head_from(ug, uag_s, uag_r, p).wait_recv())
    u_prev_send = rdma(ug.at[pl.ds(12, 4)], uvp, ups, upr, (nxt, h))
    u_prev_send.start()
    for b in range(4):
        uq[b] = jnp.concatenate([ug[2 * b], ug[2 * b + 1]], axis=1)
        uv[b] = jnp.concatenate([ug[8 + 2 * b], ug[9 + 2 * b]], axis=1)

    kv_send.wait_recv()
    fwd = rdma(kvprev.at[core], kvprev.at[core], fws, fwr, (c, sib))
    fwd.start()

    for hd in range(heads):
        up_h = quv[:, HEAD_SIZE * hd:HEAD_SIZE * (hd + 1)]
        for b in range(4):
            q_t = qt[hd, b].astype(F32) + adapter_scale * tn(up_h, uq[b])
            qt[hd, b] = turned(q_t, tc[b], ts[b]).astype(BF)

    def value_block(raw, b):
        vv[b] = (raw.astype(F32) + adapter_scale * tn(uv[b], vul[...])).astype(BF)

    for b in range(4):
        value_block(kvown[1, BLK * b:BLK * b + BLK], b)

    scale = HEAD_SIZE ** -0.5
    sharp = scale * LOG2E
    key_at = lax.broadcasted_iota(jnp.int32, (BLK, BLK), 0)
    row_at = lax.broadcasted_iota(jnp.int32, (BLK, BLK), 1)

    def chunk(hd, qi, blocks):
        q_t, d_t = qt[hd, qi], dt[hd, qi]
        d_n = dn[hd, qi]
        scores = [nn(kk[kb], q_t) for kb in blocks]
        scores[-1] = jnp.where(key_at <= row_at, scores[-1], -1e30)
        peak = functools.reduce(jnp.maximum, [jnp.max(s, axis=0, keepdims=True) for s in scores])
        peak = peak * sharp
        weights = [jnp.exp2(s * sharp - peak) for s in scores]
        total = functools.reduce(jnp.add, [jnp.sum(w, axis=0, keepdims=True) for w in weights])
        inverse = 1.0 / total
        probs = [w * inverse for w in weights]
        prob_grad = [nn(vv[kb], d_t) for kb in blocks]
        delta = functools.reduce(
            jnp.add, [jnp.sum(p * g, axis=0, keepdims=True) for p, g in zip(probs, prob_grad)]
        )
        dvs = [nn(p.astype(BF), d_n) for p in probs]
        score_grad = [(p * (g - delta)).astype(BF) for p, g in zip(probs, prob_grad)]
        dq = functools.reduce(jnp.add, [nn(kt[kb], s) for kb, s in zip(blocks, score_grad)])
        pg = turned_back(dq, tc[qi], ts[qi]).astype(BF)
        up_h = quv[:, pl.ds(pl.multiple_of(hd * HEAD_SIZE, HEAD_SIZE), HEAD_SIZE)]
        return nn(up_h, pg), nt(uq[qi], pg), dvs

    @pl.loop(0, heads)
    def _(hd):
        shifted = msk[hd]
        on = shifted.astype(F32)
        off = 1.0 - on
        q0 = 2 * shifted
        t0, a0, d0 = chunk(hd, q0, [q0])
        t1, a1, d1 = chunk(hd, q0 + 1, [q0, q0 + 1])
        qacc[hd] = a0 + a1
        tq[0] += t0 * off
        tq[1] += t1 * off
        tq[2] += t0 * on
        tq[3] += t1 * on
        x0, x1 = d0[0] + d1[0], d1[1]
        dv[0] += x0 * off
        dv[1] += x1 * off
        dv[2] += x0 * on
        dv[3] += x1 * on

    rdma(kvprev.at[1 - core], kvprev.at[1 - core], fws, fwr, (c, sib)).wait_recv()
    for j in range(2):
        key_block(kvprev[0, BLK * j:BLK * j + BLK], 4 + j, tcp[j], tsp[j])
    u_prev_send.wait_recv()
    for j in range(2):
        uv[4 + j] = jnp.concatenate([uvp[2 * j], uvp[2 * j + 1]], axis=1)
        value_block(kvprev[1, BLK * j:BLK * j + BLK], 4 + j)

    @pl.loop(0, heads)
    def _(hd):
        shifted = msk[hd]
        on = shifted.astype(F32)
        off = 1.0 - on
        q0 = 2 - 2 * shifted
        far = 4 * shifted
        t0, a0, d0 = chunk(hd, q0, [far, far + 1, q0])
        t1, a1, d1 = chunk(hd, q0 + 1, [far, far + 1, q0, q0 + 1])
        qacc[hd] += a0 + a1
        tq[0] += t0 * on
        tq[1] += t1 * on
        tq[2] += t0 * off
        tq[3] += t1 * off
        f0, f1 = d0[0] + d1[0], d0[1] + d1[1]
        x0, x1 = d0[2] + d1[2], d1[3]
        dv[0] += x0 * on + f0 * off
        dv[1] += x1 * on + f1 * off
        dv[2] += x0 * off
        dv[3] += x1 * off
        dv[4] += f0 * on
        dv[5] += f1 * on

    v_acc = jnp.zeros((16, HEAD_SIZE), F32)
    for b in range(6):
        dv_b = dv[b].astype(BF)
        t_v = (adapter_scale * nt(vul[...], dv_b)).astype(BF)
        v_acc = v_acc + nn(uv[b], dv_b)
        tsend[8 + 2 * b] = t_v[:, :128]
        tsend[9 + 2 * b] = t_v[:, 128:]
    for b in range(4):
        t_q = (adapter_scale * scale * tq[b]).astype(BF)
        tsend[2 * b] = t_q[:, :128]
        tsend[2 * b + 1] = t_q[:, 128:]

    def prev_send(k):
        return rdma(tsend.at[16 + k], tprev.at[h], tps_s.at[k], tps_r.at[h], (prv, 12 + k))

    for k in range(4):
        prev_send(k).start()
    each(nh, h, lambda p: head_rs(tsend, trecv, trs_s, trs_r, p).start())

    for l in range(heads):
        a = adapter_scale * scale * qacc[l]
        es[l] = a[:8]
        es[4 + l] = a[8:]
    es[8] = adapter_scale * v_acc[:8]
    es[9] = adapter_scale * v_acc[8:]

    def ctx_rs(src, dst, ssem, rsem, p):
        return rdma(src.at[pl.ds(p * m, m)], dst.at[c], ssem.at[p], rsem.at[c], (p, h))

    def ctx_ag(src, dst, ssem, rsem, p):
        return rdma(src, dst.at[pl.ds(c * m, m)], ssem.at[p], rsem.at[c], (p, h))

    def ctx_piece_from(dst, ssem, rsem, p):
        return rdma(dst.at[pl.ds(p * m, m)], dst.at[pl.ds(p * m, m)], ssem.at[p], rsem.at[p], (p, h))

    def if_early(p, f):
        @pl.when(p * m < 10)
        def _():
            f(p)

    each(nc, c, lambda p: if_early(p, lambda p: ctx_rs(es, er, ers_s, ers_r, p).start()))

    trecv[h] = tsend[h]
    each(nh, h, lambda p: head_from(trecv, trs_s, trs_r, p).wait_recv())
    t_sum = trecv[0].astype(F32)
    for p in range(1, 16):
        t_sum = t_sum + trecv[p].astype(F32)

    @pl.when(h < 12)
    def _():
        tsum[...] = t_sum.astype(BF)

    @pl.when(h >= 12)
    def _():
        @pl.loop(0, nh)
        def _(p):
            rdma(tprev.at[p], tprev.at[p], tps_s.at[0], tps_r.at[p], (nxt, p)).wait_recv()

        extra = t_sum
        for p in range(16):
            extra = extra + tprev[p].astype(F32)
        tsum[...] = extra.astype(BF)

    tg[h] = tsum[...]
    each(nh, h, lambda p: head_ag(tsum, tg, tag_s, tag_r, p).start())

    def early_sum(p):
        er[p] = es[pl.ds(p * m, m)]
        each(nc, c, lambda p: ctx_from(er, ers_s, ers_r, p).wait_recv())
        e_sum = er[0]
        for j in range(1, nc):
            e_sum = e_sum + er[j]
        esum[...] = e_sum
        eg[pl.ds(p * m, m)] = e_sum
        each(nc, c, lambda p: ctx_ag(esum, eg, eag_s, eag_r, p).start())

    if_early(c, early_sum)

    each(nh, h, lambda p: head_from(tg, tag_s, tag_r, p).wait_recv())
    t_all = jnp.concatenate(
        [
            jnp.concatenate([tg[8 * r + l] for l in range(8)], axis=1)
            for r in range(2)
        ],
        axis=0,
    )
    grad = nn(t_all, hidv[...])
    for p in range(16):
        r, l = p // 4, p % 4
        gs[p] = grad[8 * r:8 * r + 8, 128 * l:128 * l + 128]
    each(nc, c, lambda p: ctx_rs(gs, gr, grs_s, grs_r, p).start())

    each(nc, c, lambda p: if_early(p, lambda p: ctx_piece_from(eg, eag_s, eag_r, p).wait_recv()))
    v_part = eg.at[pl.ds(8, 2)]
    each(nh, h, lambda p: head_ag(v_part, vg, vag_s, vag_r, p).start())
    for l in range(heads):
        o_qu[:8, 128 * l:128 * l + 128] = eg[l]
        o_qu[8:, 128 * l:128 * l + 128] = eg[4 + l]
    vg[h] = eg[8:10]

    gr[c] = gs[pl.ds(c * m, m)]
    each(nc, c, lambda p: ctx_from(gr, grs_s, grs_r, p).wait_recv())
    g_sum = gr[0]
    for j in range(1, nc):
        g_sum = g_sum + gr[j]
    gsum[...] = g_sum
    gg[pl.ds(c * m, m)] = g_sum
    each(nc, c, lambda p: ctx_ag(gsum, gg, gag_s, gag_r, p).start())

    each(nh, h, lambda p: head_from(vg, vag_s, vag_r, p).wait_recv())
    per = nh // KEY_VALUE_HEADS
    for k in range(KEY_VALUE_HEADS):
        s = vg[k * per]
        for j in range(1, per):
            s = s + vg[k * per + j]
        o_vu[:8, 128 * k:128 * k + 128] = s[0]
        o_vu[8:, 128 * k:128 * k + 128] = s[1]

    kv_send.wait_send()
    fwd.wait_send()
    u_prev_send.wait_send()
    for k in range(4):
        prev_send(k).wait_send()

    def head_sent(p):
        head_rs(ub, ur, urs_s, urs_r, p).wait_send()
        head_ag(us, ug, uag_s, uag_r, p).wait_send()
        head_rs(tsend, trecv, trs_s, trs_r, p).wait_send()
        head_ag(tsum, tg, tag_s, tag_r, p).wait_send()
        head_ag(v_part, vg, vag_s, vag_r, p).wait_send()

    each(nh, h, head_sent)

    def ctx_sent(p):
        if_early(p, lambda p: ctx_rs(es, er, ers_s, ers_r, p).wait_send())
        ctx_rs(gs, gr, grs_s, grs_r, p).wait_send()
        ctx_ag(gsum, gg, gag_s, gag_r, p).wait_send()

    each(nc, c, ctx_sent)
    if_early(c, lambda _: each(nc, c, lambda p: ctx_ag(esum, eg, eag_s, eag_r, p).wait_send()))

    each(nc, c, lambda p: ctx_piece_from(gg, gag_s, gag_r, p).wait_recv())
    for p in range(16):
        r, l = p // 4, p % 4
        out = o_aq if r < 2 else o_av
        out[8 * (r % 2):8 * (r % 2) + 8, 128 * l:128 * l + 128] = gg[p]


def on_device(nc, nh, hidden, qf, kp, vf, qd, qu, vd, vu, dog, mask):
    rows, width = hidden.shape
    heads = mask.shape[0]
    m = 16 // nc
    half = rows // 2
    fine_c, fine_s, coarse_c, coarse_s = angle_tables(rows, nc)
    vm = pltpu.VMEM
    dma = pltpu.SemaphoreType.DMA
    hsem, csem = dma((nh,)), dma((nc,))
    any_spec = pl.BlockSpec(memory_space=pl.ANY)
    vmem_spec = pl.BlockSpec(memory_space=pltpu.VMEM)
    out = pl.pallas_call(
        functools.partial(kernel, nc, nh, heads),
        out_shape=(
            jax.ShapeDtypeStruct((16, width), F32),
            jax.ShapeDtypeStruct((16, width), F32),
            jax.ShapeDtypeStruct((16, width), F32),
            jax.ShapeDtypeStruct((16, KEY_VALUE_HEADS * HEAD_SIZE), F32),
        ),
        in_specs=[any_spec] * 9 + [pl.BlockSpec(memory_space=pltpu.SMEM)] + [any_spec] * 4,
        out_specs=(vmem_spec,) * 4,
        scratch_shapes=[
            vm((rows, width), BF), vm((rows, width), BF), vm((rows, width), BF),
            vm((2, rows, HEAD_SIZE), BF), vm((2, half, HEAD_SIZE), BF),
            vm((2, 16, width), BF), vm((16, width), BF), vm((16, HEAD_SIZE), BF),
            vm((HALF_HEAD, rows), F32), vm((HALF_HEAD, rows), F32),
            vm((HALF_HEAD, 128), F32), vm((HALF_HEAD, 128), F32),
            vm((16, 16, 128), F32), vm((16, 16, 128), F32), vm((16, 128), BF),
            vm((16, 16, 128), BF), vm((4, 16, 128), BF),
            vm((heads, 4, HEAD_SIZE, BLK), BF), vm((heads, 4, HEAD_SIZE, BLK), BF),
            vm((heads, 4, BLK, HEAD_SIZE), BF),
            vm((6, BLK, HEAD_SIZE), BF), vm((6, HEAD_SIZE, BLK), BF), vm((6, BLK, HEAD_SIZE), BF),
            vm((4, HALF_HEAD, BLK), F32), vm((4, HALF_HEAD, BLK), F32),
            vm((2, HALF_HEAD, BLK), F32), vm((2, HALF_HEAD, BLK), F32),
            vm((4, 16, BLK), BF), vm((6, 16, BLK), BF),
            vm((4, 16, BLK), F32), vm((heads, 16, HEAD_SIZE), F32), vm((6, BLK, HEAD_SIZE), F32),
            vm((20, 16, 128), BF), vm((16, 16, 128), BF), vm((16, 16, 128), BF),
            vm((16, 128), BF), vm((16, 16, 128), BF),
            vm((16, 8, 128), F32), vm((nc, m, 8, 128), F32), vm((m, 8, 128), F32),
            vm((16, 8, 128), F32), vm((16, 2, 8, 128), F32),
            vm((16, 8, 128), F32), vm((nc, m, 8, 128), F32), vm((m, 8, 128), F32), vm((16, 8, 128), F32),
            dma((13,)), dma, dma, dma, dma, dma, dma,
            hsem, hsem, hsem, hsem, hsem, hsem, dma((4,)), hsem, hsem, hsem,
            csem, csem, csem, csem, hsem, hsem, csem, csem, csem, csem,
        ],
        compiler_params=pltpu.CompilerParams(
            collective_id=0, has_side_effects=True, vmem_limit_bytes=56 * 1024 * 1024
        ),
        name="adapter_grads",
    )(hidden, qf, kp, vf, qd.T, qu, vd.T, vu, dog, mask, fine_c, fine_s, coarse_c, coarse_s)
    a_q, q_up, a_v, v_up = out
    return a_q.T, q_up, a_v.T, v_up


def solution(mesh):
    nc, nh = mesh.shape["ctx"], mesh.shape["head"]
    return jax.shard_map(
        functools.partial(on_device, nc, nh),
        mesh=mesh,
        in_specs=(
            P("ctx", "head"),
            P("ctx", "head"),
            P("ctx", None),
            P("ctx", None),
            P("head", None),
            P(None, "head"),
            P("head", None),
            P(),
            P("ctx", "head"),
            P("head"),
        ),
        out_specs=(P("head", None), P(None, "head"), P("head", None), P()),
        check_vma=False,
    )
```

time: 590 us -> 68.6 us (0.12)
  waiting for transfers between devices: 342 us -> 0 us
  blocking collectives: 114 us -> 0 us
  Pallas kernels: 0 us -> 62 us
  matrix products: 41.3 us -> 0 us
  local copies, waits for them, and re-layouts: 34.7 us -> 5.6 us
  other arithmetic: 25.5 us -> 0 us
  starting transfers between devices: 16.6 us -> 0 us
  between operations: 14.4 us -> 0.64 us
    psum x2 -> x0, waiting for transfers between devices: 317 us -> none  [the longest x1 159 us: on_device(): lax.psum((a_q_part, a_v_part, query_up_gradient_piece), 'ctx')]
    psum x2 -> x0, blocking collectives: 114 us -> none  [the longest x1 61.3 us: on_device(): lax.psum((token_query_piece, token_value_piece), 'head')]
    pallas_call x0 -> x1, Pallas kernels: none -> 62 us  [on_device(): pl.pallas_call(functools.partial(kernel, nc, nh, heads), out_shape=(jax.S...]
    dot_general x26 -> x0, matrix products: 41.3 us -> none  [the longest x4 15.8 us: group_grads(): jnp.dot(score_grad, key_rows, preferred_element_type=jnp.float32)]
    ppermute x6 -> x0, waiting for transfers between devices: 25.2 us -> none  [passed_along(): return lax.ppermute(block, axis, route)]
    ppermute x6 -> x0, starting transfers between devices: 16.3 us -> none  [passed_along(): return lax.ppermute(block, axis, route)]
    reduce_sum x6 -> x0, other arithmetic: 6.69 us -> none  [the longest x1 3.81 us: on_device(): send_value.reshape(local_key_value_heads, fan_out, half_rows, HEAD_SIZE)]
  transfers between devices with their start and end apart: 8 -> 0, of which waited for: 5 -> 0; matrix products, arithmetic and copies ran while one was open for 6% -> 0% of each run, Pallas kernels for 0% -> 0%
where the time goes in v1:
time: 68.6 us; the launch traced here: 68.3 us
  Pallas kernels  62 us (90%)
  local copies, waits for them, and re-layouts  5.6 us (8%)
    pallas_call x1, Pallas kernels, on_device(): pl.pallas_call(functools.partial(kernel, nc, nh, heads), out_shape=(jax.S...  62 us
    unnamed x4, local copies, waits for them, and re-layouts  5.6 us

profile of v1, /device:TPU:8, one launch (start us, length us, event | category | flops | bytes accessed | tf_op | source)
XLA Modules:
  0.0 68.3 jit_solution(17541948048641336547)
XLA Ops:
  0.6 62.0 %adapter_grads.1 = (f32[16,512]{1,0:T(8,128)}, f32[16,512]{1,0:T(8,128)}, f32[16,512]{1,0:T(8,128)}, f32[16,1024]{1,0:T(8,128)}) custom-call(bf16[1024,512]{1,0:T(8,128)(2,1)} %hid.1, bf16[1024,512]{1,0:T(8,128)(2,1)} %qf.1, bf16[1024,1024]{1,0:T(8,128)(2,1)} %kp.1, bf16[1024,1024]{1,0:T(8,128)(2,1)} %vf.1, bf16[16,512]{1,0:T(8,128)(2,1)} %bitcast.6, ...), custom_call_target="tpu_custom_call" | custom-call | tf_op jit(solution)/shard_map/adapter_grads/pallas_call | solution.py:450
  62.7 1.4 %copy.22 = f32[512,16]{0,1:T(8,128)} copy(f32[512,16]{0,1:T(8,128)} %bitcast.5) | data formatting | bytes 65536
  64.0 1.4 %copy.23 = f32[16,512]{1,0:T(8,128)} copy(f32[16,512]{1,0:T(8,128)} %get-tuple-element.17) | data formatting | bytes 65536
  65.4 1.4 %copy.24 = f32[512,16]{0,1:T(8,128)} copy(f32[512,16]{0,1:T(8,128)} %bitcast.4) | data formatting | bytes 65536
  66.8 1.5 %copy.25 = f32[16,1024]{1,0:T(8,128)} copy(f32[16,1024]{1,0:T(8,128)} %get-tuple-element.19) | data formatting | bytes 131072
